TPU v7x, 32 devices: a whole 2x2x4 slice. The times are simulated.
32 devices in a mesh: grp: 4 (over y, x), line: 8 (over z, core).
Axes of the slice: x: 2, y: 2, z: 4, core: 2. Of those that a mesh axis runs over, the one named last changes fastest.
Arguments:
- velocity: bfloat16 [3, 1536, 96, 512], P(None, 'line', 'grp'), may hold values from -6 to 6
- vorticity: bfloat16 [3, 1536, 96, 512], P(None, 'line', 'grp'), may hold values from -6 to 6
- wall_velocity: float32 [2, 256, 96, 1536], P(None, ('grp', 'line')), may hold values from -6 to 6
- wall_vorticity: float32 [2, 256, 96, 1536], P(None, ('grp', 'line')), may hold values from -6 to 6
- keep_mask: int32 [256, 96], P(('grp', 'line')), may hold values from 0 to 1, as said below
- derivative_band: float32 [7, 1536], replicated, may hold values from -3 to 3
- eigenvalues: float32 [1536], replicated, may hold values from 0.25 to 4
- eigenbasis: float32 [1536, 1536], replicated, may hold values from -0.15625 to 0.15625
Outputs:
- new_velocity: float32 [2, 256, 96, 1536], P(None, ('grp', 'line'))
- new_vorticity: float32 [2, 256, 96, 1536], P(None, ('grp', 'line'))
Inputs may be any that keep to these rules, and one draw needn't show every extreme that they name: keep_mask is 0 wherever kx >= 170, or 32 <= kz < 64.
All inputs are finite; a program needn't handle non-finite values.
Results may differ from a plain program's by a relative error of at most 0.0003.
Values sent between devices are 32-bit elements; how exact they have to be, the bound alone decides.
A program may use at most 384 MiB of HBM per device.

v0:
```python
import math
import jax
import jax.numpy as jnp
from jax import lax
from jax.sharding import PartitionSpec as P

HIGHEST_PRECISION = lax.Precision.HIGHEST


def phase_table(indices, points):
    index_cols = jnp.arange(points, dtype=jnp.int32)[None, :]
    phase_angle = (indices[:, None] * index_cols % points).astype(jnp.float32) * (
        2.0 * math.pi / points
    )
    norm_scale = 1.0 / math.sqrt(points)
    return (jnp.cos(phase_angle) * norm_scale, jnp.sin(phase_angle) * norm_scale)


def signed_wave(indices, points):
    signed_index = jnp.where(indices < points // 2, indices, indices - points)
    return signed_index.astype(jnp.float32) / (points / 2.0)


def curl_terms(spectra, stream_wave, span_wave):
    slope_source = jnp.stack(
        [
            -stream_wave * spectra[0, 1] - span_wave * spectra[2, 1],
            stream_wave * spectra[0, 0] + span_wave * spectra[2, 0],
        ]
    )
    normal_term = jnp.stack(
        [
            -span_wave * spectra[0, 1] + stream_wave * spectra[2, 1],
            span_wave * spectra[0, 0] - stream_wave * spectra[2, 0],
        ]
    )
    return (slope_source, normal_term)


def banded(padded, band_rows, extent):
    summed = band_rows[0] * padded[..., 0:extent]
    for offset in range(1, 7):
        summed = summed + band_rows[offset] * padded[..., offset : offset + extent]
    return summed


def local(
    velocity,
    vorticity,
    wall_velocity,
    wall_vorticity,
    keep_mask,
    derivative_band,
    eigenvalues,
    eigenbasis,
):
    group_count = lax.axis_size("grp")
    line_count = lax.axis_size("line")
    group_index = lax.axis_index("grp")
    line_index = lax.axis_index("line")
    moving = velocity.astype(jnp.float32)
    turning = vorticity.astype(jnp.float32)
    lamb_vector = jnp.stack(
        [
            moving[1] * turning[2] - moving[2] * turning[1],
            moving[2] * turning[0] - moving[0] * turning[2],
            moving[0] * turning[1] - moving[1] * turning[0],
        ]
    )
    slab_depth = lamb_vector.shape[1]
    span_share = lamb_vector.shape[2]
    stream_points = lamb_vector.shape[3]
    span_points = span_share * group_count
    stream_modes = stream_points // 2
    group_modes = stream_modes // group_count
    line_modes = group_modes // line_count
    span_keep = span_points // 3
    wall_points = wall_velocity.shape[3]
    span_list = jnp.concatenate(
        [
            jnp.arange(span_keep, dtype=jnp.int32),
            jnp.arange(span_points - span_keep, span_points, dtype=jnp.int32),
        ]
    )
    span_count = span_list.shape[0]
    stream_cosine, stream_sine = phase_table(
        jnp.arange(stream_modes, dtype=jnp.int32), stream_points
    )
    stream_table = jnp.stack(
        [
            stream_cosine.reshape(group_count, group_modes, stream_points),
            -stream_sine.reshape(group_count, group_modes, stream_points),
        ],
        1,
    )
    stream_table = stream_table.reshape(2 * stream_modes, stream_points)
    stream_spectra = jnp.einsum(
        "rx,cx->rc",
        lamb_vector.reshape(-1, stream_points),
        stream_table,
        precision=HIGHEST_PRECISION,
    )
    stream_spectra = stream_spectra.reshape(3, slab_depth, span_share, 2 * stream_modes)
    span_cosine, span_sine = phase_table(span_list, span_points)
    planes = lax.all_to_all(stream_spectra, "grp", split_axis=3, concat_axis=2, tiled=True)
    count_items = planes.shape[1]
    cosine_part = jnp.einsum("qz,fnzc->fcqn", span_cosine, planes, precision=HIGHEST_PRECISION)
    sine_part = jnp.einsum("qz,fnzc->fcqn", span_sine, planes, precision=HIGHEST_PRECISION)
    cosine_part = cosine_part.reshape(3, 2, group_modes, span_count, count_items)
    sine_part = sine_part.reshape(3, 2, group_modes, span_count, count_items)
    real_part = cosine_part[:, 0] + sine_part[:, 1]
    imag_part = cosine_part[:, 1] - sine_part[:, 0]
    local_modes = jnp.stack([real_part, imag_part], 1)
    span_wave = signed_wave(span_list, span_points)[:, None]
    device_modes = (group_index * line_count + line_index) * line_modes + jnp.arange(
        line_modes, dtype=jnp.int32
    )
    device_wave = (device_modes.astype(jnp.float32) / stream_modes)[:, None, None]
    whole_lines = lax.all_to_all(local_modes, "line", split_axis=2, concat_axis=4, tiled=True)
    wave_square = device_wave * device_wave + span_wave * span_wave
    slope_source, normal_term = curl_terms(whole_lines, device_wave, span_wave)
    padded = jnp.pad(slope_source, ((0, 0), (0, 0), (0, 0), (3, 3)))
    arrived = jnp.stack(
        [wave_square * whole_lines[1] - banded(padded, derivative_band, wall_points), normal_term]
    )
    middle = jnp.zeros((2, 2, line_modes, span_points - 2 * span_keep, wall_points), jnp.float32)
    arrived = jnp.concatenate(
        [arrived[:, :, :, :span_keep], middle, arrived[:, :, :, span_keep:]], 3
    )
    keep_weight = keep_mask.astype(jnp.float32)[:, :, None]
    right_side = jnp.stack([wall_velocity, wall_vorticity]) + keep_weight * arrived
    full_wave = signed_wave(jnp.arange(span_points, dtype=jnp.int32), span_points)[:, None]
    full_square = device_wave * device_wave + full_wave * full_wave
    eigen_coeffs = jnp.einsum(
        "fpkqy,yj->fpkqj", right_side, eigenbasis, precision=HIGHEST_PRECISION
    )
    eigen_coeffs = eigen_coeffs / (eigenvalues + full_square)
    solved = jnp.einsum("fpkqj,yj->fpkqy", eigen_coeffs, eigenbasis, precision=HIGHEST_PRECISION)
    return (solved[0], solved[1])


def solution(mesh):
    placed = (
        P(None, "line", "grp", None),
        P(None, "line", "grp", None),
        P(None, ("grp", "line"), None, None),
        P(None, ("grp", "line"), None, None),
        P(("grp", "line"), None),
        P(),
        P(),
        P(),
    )
    return jax.shard_map(
        local,
        mesh=mesh,
        in_specs=placed,
        out_specs=(P(None, ("grp", "line"), None, None), P(None, ("grp", "line"), None, None)),
        check_vma=False,
    )
```

profile of v0, /device:TPU:0, one launch (start us, length us, event | category | flops | bytes accessed | tf_op | source)
XLA Modules:
  0.0 1655.5 jit_solution(10274515562087793496)
XLA Ops:
  0.7 17.1 %convert_element_type.71 = f32[3,192,24,512]{3,2,1,0:T(8,128)} convert(bf16[3,192,24,512]{3,2,1,0:T(8,128)(2,1)} %param.8) | non-fusion elementwise | flops 7077888 | bytes 42467328 | tf_op jit(solution)/shard_map/convert_element_type | solution.py:61
  20.1 10.3 convert_element_type.72
  32.6 30.8 %multiply_subtract_fusion.2 = (f32[1,192,24,512]{3,2,1,0:T(8,128)}, f32[1,192,24,512]{3,2,1,0:T(8,128)}, f32[1,192,24,512]{3,2,1,0:T(8,128)}) fusion(f32[3,192,24,512]{3,2,1,0:T(8,128)} %convert_element_type.72, f32[3,192,24,512]{3,2,1,0:T(8,128)} %convert_element_type.71), kind=kLoop, calls=%fused_computation.37 | loop fusion | flops 21233664 | bytes 84934656 | tf_op jit(solution)/shard_map/sub | solution.py:65
  63.5 51.6 %fusion = f32[3,192,24,512]{3,2,1,0:T(8,128)} fusion(f32[512,512,1,1]{1,0,3,2:T(8,128)S(1)} %bitcast.85, f32[1,192,24,512]{3,2,1,0:T(8,128)} %get-tuple-element.14, f32[1,192,24,512]{3,2,1,0:T(8,128)} %get-tuple-element.13, f32[1,192,24,512]{3,2,1,0:T(8,128)} %get-tuple-element.12), kind=kOutput, calls=%fused_computation | convolution fusion | flops 43500699648 | bytes 57671680 | tf_op jit(solution)/shard_map/rx,cx->rc/dot_general | solution.py:97
  115.1 36.9 %copy.28 = f32[3,192,24,512]{1,2,0,3:T(8,128)} copy(f32[3,192,24,512]{3,2,1,0:T(8,128)} %fusion) | data formatting | bytes 56623104 | tf_op jit(solution)/shard_map/rx,cx->rc/dot_general | solution.py:97
  152.0 11.0 all-to-all-start
  163.1 408.4 %all-to-all-done = f32[3,192,24,512]{1,2,0,3:T(8,128)} async-done(((f32[3,192,24,512]{1,2,0,3:T(8,128)}), f32[3,192,24,512]{1,2,0,3:T(8,128)}, u32[]{:S(2)}, u32[]{:S(2)}) %all-to-all-start) | async-done | bytes 28311584 | tf_op jit(solution)/shard_map/all_to_all | solution.py:105
  571.6 34.4 %copy.29 = f32[3,192,24,4,128]{4,2,3,1,0:T(8,128)} copy(f32[3,192,24,4,128]{1,2,0,4,3:T(8,128)} %bitcast.5) | data formatting | bytes 56623104 | tf_op jit(solution)/shard_map/all_to_all | solution.py:105
  606.0 26.2 %convolution_bitcast_fusion.1 = f32[3,128,64,192]{1,2,3,0:T(8,128)} fusion(f32[3,192,96,128]{3,2,1,0:T(8,128)} %bitcast.80, s32[64]{0:T(128)S(1)} %get-tuple-element.11), kind=kOutput, calls=%fused_computation.40 | convolution fusion | flops 5435879424 | bytes 47186176 | tf_op jit(solution)/shard_map/qz,fnzc->fcqn/dot_general | solution.py:107
  632.3 26.2 %convolution_bitcast_fusion = f32[3,128,64,192]{1,2,3,0:T(8,128)} fusion(f32[3,192,96,128]{3,2,1,0:T(8,128)} %bitcast.81, s32[64]{0:T(128)S(1)} %get-tuple-element.11), kind=kOutput, calls=%fused_computation.39 | convolution fusion | flops 5435879424 | bytes 47186176 | tf_op jit(solution)/shard_map/qz,fnzc->fcqn/dot_general | solution.py:108
  658.4 25.1 %copy.30 = f32[3,128,64,192]{3,2,1,0:T(8,128)} copy(f32[3,128,64,192]{1,2,3,0:T(8,128)} %convolution_bitcast_fusion.1) | data formatting | bytes 37748736 | tf_op jit(solution)/shard_map/qz,fnzc->fcqn/transpose | solution.py:107
  683.5 25.1 %copy.31 = f32[3,128,64,192]{3,2,1,0:T(8,128)} copy(f32[3,128,64,192]{1,2,3,0:T(8,128)} %convolution_bitcast_fusion) | data formatting | bytes 37748736 | tf_op jit(solution)/shard_map/qz,fnzc->fcqn/transpose | solution.py:108
  708.6 27.5 %slice_add_fusion = (f32[3,1,64,64,192]{4,3,2,1,0:T(8,128)}, f32[3,1,64,64,192]{4,3,2,1,0:T(8,128)}) fusion(f32[3,2,64,64,192]{4,3,2,1,0:T(8,128)} %bitcast.83, f32[3,2,64,64,192]{4,3,2,1,0:T(8,128)} %bitcast.82), kind=kLoop, calls=%fused_computation.24 | loop fusion | flops 4718592 | bytes 56623104 | tf_op jit(solution)/shard_map/add | solution.py:111
  736.1 9.4 pad_maximum_fusion
  745.5 8.6 copy.32
  754.2 6.6 all-to-all-start.1
  761.2 2.6 broadcast_add_fusion
  763.7 540.4 %all-to-all-done.1 = f32[3,2,64,64,192]{4,3,1,0,2:T(8,128)} async-done(((f32[3,2,64,64,192]{4,3,1,0,2:T(8,128)}), f32[3,2,64,64,192]{4,3,1,0,2:T(8,128)}, u32[]{:S(2)}, u32[]{:S(2)}) %all-to-all-start.1) | async-done | bytes 18874400 | tf_op jit(solution)/shard_map/all_to_all | solution.py:119
  1304.1 26.5 %copy.35 = f32[3,2,8,64,8,192]{5,4,3,2,1,0:T(8,128)} copy(f32[3,2,8,64,8,192]{5,3,1,0,2,4:T(8,128)} %bitcast.20) | data formatting | bytes 37748736 | tf_op jit(solution)/shard_map/all_to_all | solution.py:119
  1330.7 25.3 %all_to_all.33 = f32[3,2,8,64,1536]{4,3,2,1,0:T(8,128)} reshape(f32[3,2,8,64,8,192]{5,4,3,2,1,0:T(8,128)} %copy.35) | data formatting | bytes 37748736 | tf_op jit(solution)/shard_map/all_to_all | solution.py:119
  1355.9 17.5 %copy.33 = f32[3,2,64,64,192]{4,3,2,1,0:T(8,128)} copy(f32[3,2,64,64,192]{4,3,1,0,2:T(8,128)} %all-to-all-done.1) | data formatting | bytes 37748736 | tf_op jit(solution)/shard_map/all_to_all | solution.py:119
  1373.5 4.0 slice.150
  1377.5 9.9 copy.34
  1387.4 9.5 squeeze.14
  1396.9 5.6 multiply_add_fusion.1
  1402.5 3.1 pad_maximum_fusion.1
  1405.6 3.1 maximum_bitcast_fusion
  1408.8 23.5 %subtract_bitcast_fusion = f32[1,2,8,64,1536]{4,3,2,1,0:T(8,128)} fusion(f32[2,8,64,1536]{3,2,1,0:T(8,128)} %pad_maximum_fusion.1, f32[2,8,64,1536]{3,2,1,0:T(8,128)} %squeeze.14, f32[1536]{0:T(1024)S(1)} %get-tuple-element.7, f32[1536]{0:T(1024)S(1)} %get-tuple-element.8, f32[1536]{0:T(1024)S(1)} %get-tuple-element.3, f32[1536]{0:T(1024)S(1)} %get-tuple-element.4, ...), kind=kLoop, calls=%fused_computation.44 | loop fusion | flops 23592960 | bytes 18919424 | tf_op jit(solution)/shard_map/stack | solution.py:123
  1432.3 6.3 fusion.28
  1438.6 105.2 %fusion.9 = f32[2,2,8,96,1536]{4,3,2,1,0:T(8,128)} fusion(f32[1,2,8,64,1536]{4,3,2,1,0:T(8,128)} %maximum_bitcast_fusion, f32[1,2,8,64,1536]{4,3,2,1,0:T(8,128)} %subtract_bitcast_fusion, f32[1,2,8,96,1536]{4,3,2,1,0:T(8,128)} %bitcast.86, f32[1,2,8,96,1536]{4,3,2,1,0:T(8,128)} %bitcast.87, f32[2,2,8,32,1536]{4,3,2,1,0:T(8,128)} %fusion.28, ...), kind=kOutput, calls=%fused_computation.11 | convolution fusion | flops 87015555072 | bytes 66063744 | tf_op jit(solution)/shard_map/fpkqy,yj->fpkqj/dot_general | solution.py:134
  1543.8 99.0 %fusion.19 = f32[2,2,8,96,1536]{4,3,2,1,0:T(8,128)} fusion(f32[2,2,8,96,1536]{4,3,2,1,0:T(8,128)} %fusion.9, f32[1536,1536]{1,0:T(8,128)} %param.15, f32[8,96,1536]{2,1,0:T(8,128)} %broadcast_add_fusion), kind=kOutput, calls=%fused_computation.21 | convolution fusion | flops 86977806336 | bytes 51904512 | tf_op jit(solution)/shard_map/fpkqj,yj->fpkqy/dot_general | solution.py:138
  1642.7 12.6 slice_bitcast_fusion
  (24 shorter events, 5.2 us)
Async XLA Ops:
  0.6 19.5 %copy-start = (bf16[3,192,24,512]{3,2,1,0:T(8,128)(2,1)S(1)}, bf16[3,192,24,512]{3,2,1,0:T(8,128)(2,1)}, u32[]{:S(2)}) copy-start(bf16[3,192,24,512]{3,2,1,0:T(8,128)(2,1)} %param.9) | copy-start | bytes 42467332
  152.0 419.6 %all-to-all-start = ((f32[3,192,24,512]{1,2,0,3:T(8,128)}), f32[3,192,24,512]{1,2,0,3:T(8,128)}, u32[]{:S(2)}, u32[]{:S(2)}) async-start(f32[3,192,24,512]{1,2,0,3:T(8,128)} %copy.28), calls=%async_computation | async-start | bytes 75497472 | tf_op jit(solution)/shard_map/all_to_all | solution.py:105
  754.2 6.6 copy-start.3
  754.2 6.7 copy-start.1
  754.2 7.0 copy-start.2
  754.2 550.0 %all-to-all-start.1 = ((f32[3,2,64,64,192]{4,3,1,0,2:T(8,128)}), f32[3,2,64,64,192]{4,3,1,0,2:T(8,128)}, u32[]{:S(2)}, u32[]{:S(2)}) async-start(f32[3,2,64,64,192]{4,3,1,0,2:T(8,128)} %copy.32), calls=%async_computation.1 | async-start | bytes 50331648 | tf_op jit(solution)/shard_map/all_to_all | solution.py:119
where the time goes:
time: 1660 us
  waiting for transfers between devices  949 us (57%)
  matrix products  308 us (19%)
  local copies, waits for them, and re-layouts  238 us (14%)
  other arithmetic  142 us (9%)
  starting transfers between devices  17.6 us (1%)
    all_to_all x1, waiting for transfers between devices, local(): lax.all_to_all(local_modes, 'line', split_axis=2, concat_axis=4, tiled=True)  540 us
    all_to_all x1, waiting for transfers between devices, local(): lax.all_to_all(stream_spectra, 'grp', split_axis=3, concat_axis=2, tiled=...  408 us
    dot_general x1, matrix products, local(): jnp.einsum('fpkqy,yj->fpkqj', right_side, eigenbasis, precision=HIGHEST_P...  105 us
    dot_general x1, matrix products, local(): jnp.einsum('fpkqj,yj->fpkqy', eigen_coeffs, eigenbasis, precision=HIGHEST...  99 us
    all_to_all x3, local copies, waits for them, and re-layouts, local(): lax.all_to_all(local_modes, 'line', split_axis=2, concat_axis=4, tiled=True)  69.3 us
    dot_general x1, matrix products, local(): jnp.einsum('rx,cx->rc', lamb_vector.reshape(-1, stream_points), stream_ta...  51.6 us
    dot_general x1, local copies, waits for them, and re-layouts, local(): jnp.einsum('rx,cx->rc', lamb_vector.reshape(-1, stream_points), stream_ta...  36.9 us
    all_to_all x1, local copies, waits for them, and re-layouts, local(): lax.all_to_all(stream_spectra, 'grp', split_axis=3, concat_axis=2, tiled=...  34.4 us
  transfers between devices with their start and end apart: 2, of which 2 were waited for; matrix products, arithmetic and copies ran while one was open for 0% of the time, Pallas kernels for 0%

commit v1 on v0

--- a/solution.py
+++ b/solution.py
@@ -116,7 +116,19 @@
         line_modes, dtype=jnp.int32
     )
     device_wave = (device_modes.astype(jnp.float32) / stream_modes)[:, None, None]
-    whole_lines = lax.all_to_all(local_modes, "line", split_axis=2, concat_axis=4, tiled=True)
+    ways, here = (lax.axis_size("line"), lax.axis_index("line"))
+    width = local_modes.shape[2] // ways
+    dims = list(local_modes.shape)
+    dims[2] = width
+    height = dims[4]
+    dims[4] = height * ways
+    full = jnp.zeros(dims, local_modes.dtype)
+    for mask in range(ways):
+        part = lax.dynamic_slice_in_dim(local_modes, (here ^ mask) * width, width, axis=2)
+        if mask:
+            part = lax.ppermute(part, "line", [(d, d ^ mask) for d in range(ways)])
+        full = lax.dynamic_update_slice_in_dim(full, part, (here ^ mask) * height, axis=4)
+    whole_lines = full
     wave_square = device_wave * device_wave + span_wave * span_wave
     slope_source, normal_term = curl_terms(whole_lines, device_wave, span_wave)
     padded = jnp.pad(slope_source, ((0, 0), (0, 0), (0, 0), (3, 3)))

time: 1660 us -> 1580 us (0.952)
  the two profiles are of different devices: /device:TPU:0 before, /device:TPU:16 now
where the time goes in v1:
time: 1580 us; the launch traced here: 1570 us
  waiting for transfers between devices  805 us (51%)
  matrix products  308 us (19%)
  local copies, waits for them, and re-layouts  289 us (18%)
  other arithmetic  151 us (10%)
  starting transfers between devices  16.1 us (1%)
    all_to_all x1, waiting for transfers between devices, local(): lax.all_to_all(stream_spectra, 'grp', split_axis=3, concat_axis=2, tiled=...  407 us
    ppermute x7, waiting for transfers between devices, local(): part = lax.ppermute(part, 'line', [(d, d ^ mask) for d in range(ways)])  398 us
    dynamic_update_slice x8, local copies, waits for them, and re-layouts, local(): lax.dynamic_update_slice_in_dim(full, part, (here ^ mask) * height, axis=4)  144 us
    dot_general x1, matrix products, local(): jnp.einsum('fpkqy,yj->fpkqj', right_side, eigenbasis, precision=HIGHEST_P...  105 us
    dot_general x1, matrix products, local(): jnp.einsum('fpkqj,yj->fpkqy', eigen_coeffs, eigenbasis, precision=HIGHEST...  99.2 us
    dot_general x1, matrix products, local(): jnp.einsum('rx,cx->rc', lamb_vector.reshape(-1, stream_points), stream_ta...  51.5 us
    dot_general x1, local copies, waits for them, and re-layouts, local(): jnp.einsum('rx,cx->rc', lamb_vector.reshape(-1, stream_points), stream_ta...  36.8 us
    all_to_all x1, local copies, waits for them, and re-layouts, local(): lax.all_to_all(stream_spectra, 'grp', split_axis=3, concat_axis=2, tiled=...  34.4 us
  transfers between devices with their start and end apart: 8, of which 6 were waited for; matrix products, arithmetic and copies ran while one was open for 9% of the time, Pallas kernels for 0%

profile of v1, /device:TPU:16, one launch (start us, length us, event | category | flops | bytes accessed | tf_op | source)
XLA Modules:
  0.0 1570.3 jit_solution(15877060042743950831)
XLA Ops:
  0.7 17.1 %convert_element_type.71 = f32[3,192,24,512]{3,2,1,0:T(8,128)} convert(bf16[3,192,24,512]{3,2,1,0:T(8,128)(2,1)} %param.8) | non-fusion elementwise | flops 7077888 | bytes 42467328 | tf_op jit(solution)/shard_map/convert_element_type | solution.py:61
  20.1 10.3 convert_element_type.72
  32.6 30.8 %multiply_subtract_fusion.2 = (f32[1,192,24,512]{3,2,1,0:T(8,128)}, f32[1,192,24,512]{3,2,1,0:T(8,128)}, f32[1,192,24,512]{3,2,1,0:T(8,128)}) fusion(f32[3,192,24,512]{3,2,1,0:T(8,128)} %convert_element_type.72, f32[3,192,24,512]{3,2,1,0:T(8,128)} %convert_element_type.71), kind=kLoop, calls=%fused_computation.52 | loop fusion | flops 21233664 | bytes 84934656 | tf_op jit(solution)/shard_map/sub | solution.py:65
  63.5 51.5 %fusion = f32[3,192,24,512]{3,2,1,0:T(8,128)} fusion(f32[512,512,1,1]{1,0,3,2:T(8,128)S(1)} %bitcast.84, f32[1,192,24,512]{3,2,1,0:T(8,128)} %get-tuple-element.14, f32[1,192,24,512]{3,2,1,0:T(8,128)} %get-tuple-element.13, f32[1,192,24,512]{3,2,1,0:T(8,128)} %get-tuple-element.12), kind=kOutput, calls=%fused_computation.16 | convolution fusion | flops 43500699648 | bytes 57671680 | tf_op jit(solution)/shard_map/rx,cx->rc/dot_general | solution.py:97
  115.1 36.8 %copy.22 = f32[3,192,24,512]{1,2,0,3:T(8,128)} copy(f32[3,192,24,512]{3,2,1,0:T(8,128)} %fusion) | data formatting | bytes 56623104 | tf_op jit(solution)/shard_map/rx,cx->rc/dot_general | solution.py:97
  151.9 10.9 all-to-all-start
  163.0 407.0 %all-to-all-done = f32[3,192,24,512]{1,2,0,3:T(8,128)} async-done(((f32[3,192,24,512]{1,2,0,3:T(8,128)}), f32[3,192,24,512]{1,2,0,3:T(8,128)}, u32[]{:S(2)}, u32[]{:S(2)}) %all-to-all-start) | async-done | bytes 28311584 | tf_op jit(solution)/shard_map/all_to_all | solution.py:105
  570.0 34.4 %copy.23 = f32[3,192,24,4,128]{4,2,3,1,0:T(8,128)} copy(f32[3,192,24,4,128]{1,2,0,4,3:T(8,128)} %bitcast.5) | data formatting | bytes 56623104 | tf_op jit(solution)/shard_map/all_to_all | solution.py:105
  604.4 26.2 %convolution_bitcast_fusion.1 = f32[3,128,64,192]{1,2,3,0:T(8,128)} fusion(f32[3,192,96,128]{3,2,1,0:T(8,128)} %bitcast.80, s32[64]{0:T(128)S(1)} %get-tuple-element.11), kind=kOutput, calls=%fused_computation.55 | convolution fusion | flops 5435879424 | bytes 47186176 | tf_op jit(solution)/shard_map/qz,fnzc->fcqn/dot_general | solution.py:107
  630.7 26.2 %convolution_bitcast_fusion = f32[3,128,64,192]{1,2,3,0:T(8,128)} fusion(f32[3,192,96,128]{3,2,1,0:T(8,128)} %bitcast.81, s32[64]{0:T(128)S(1)} %get-tuple-element.11), kind=kOutput, calls=%fused_computation.54 | convolution fusion | flops 5435879424 | bytes 47186176 | tf_op jit(solution)/shard_map/qz,fnzc->fcqn/dot_general | solution.py:108
  656.8 25.1 %copy.24 = f32[3,128,64,192]{3,2,1,0:T(8,128)} copy(f32[3,128,64,192]{1,2,3,0:T(8,128)} %convolution_bitcast_fusion.1) | data formatting | bytes 37748736 | tf_op jit(solution)/shard_map/qz,fnzc->fcqn/transpose | solution.py:107
  681.9 25.1 %copy.25 = f32[3,128,64,192]{3,2,1,0:T(8,128)} copy(f32[3,128,64,192]{1,2,3,0:T(8,128)} %convolution_bitcast_fusion) | data formatting | bytes 37748736 | tf_op jit(solution)/shard_map/qz,fnzc->fcqn/transpose | solution.py:108
  707.0 27.5 %slice_subtract_fusion = (f32[3,1,64,64,192]{4,3,2,1,0:T(8,128)}, f32[3,1,64,64,192]{4,3,2,1,0:T(8,128)}) fusion(f32[3,2,64,64,192]{4,3,2,1,0:T(8,128)} %bitcast.83, f32[3,2,64,64,192]{4,3,2,1,0:T(8,128)} %bitcast.82), kind=kLoop, calls=%fused_computation.38 | loop fusion | flops 4718592 | bytes 56623104 | tf_op jit(solution)/shard_map/sub | solution.py:112
  734.5 11.7 fusion.38
  748.3 6.6 fusion.45
  757.8 191.0 %collective-permute-done.1 = f32[3,2,8,64,192]{4,3,2,1,0:T(8,128)} collective-permute-done((f32[3,2,8,64,192]{4,3,2,1,0:T(8,128)}, f32[3,2,8,64,192]{4,3,2,1,0:T(8,128)}, u32[]{:S(2)}, u32[]{:S(2)}) %collective-permute-start.1) | collective-permute-done | bytes 2359328 | tf_op jit(solution)/shard_map/ppermute | solution.py:129
  951.8 8.9 broadcast_in_dim.4
  960.6 15.2 dynamic_update_slice.24
  975.9 20.3 %dynamic_update_slice.25 = f32[3,2,8,64,1536]{4,3,2,1,0:T(8,128)} dynamic-update-slice(f32[3,2,8,64,1536]{4,3,2,1,0:T(8,128)} %dynamic_update_slice.24, f32[3,2,8,64,192]{4,3,2,1,0:T(8,128)} %collective-permute-done, s32[]{:T(128)} %constant.75.clone.1, s32[]{:T(128)} %constant.75.clone.1, s32[]{:T(128)} %constant.75.clone.1, s32[]{:T(128)} %constant.75.clone.1, s32[]{:T(128)S(6)} %select_n.107) | dynamic-update-slice | bytes 4718596 | tf_op jit(solution)/shard_map/dynamic_update_slice | solution.py:130
  996.2 15.7 dynamic_update_slice.26
  1015.6 19.6 %dynamic_update_slice.27 = f32[3,2,8,64,1536]{4,3,2,1,0:T(8,128)} dynamic-update-slice(f32[3,2,8,64,1536]{4,3,2,1,0:T(8,128)} %dynamic_update_slice.26, f32[3,2,8,64,192]{4,3,2,1,0:T(8,128)} %collective-permute-done.2, s32[]{:T(128)} %constant.75.clone.1, s32[]{:T(128)} %constant.75.clone.1, s32[]{:T(128)} %constant.75.clone.1, s32[]{:T(128)} %constant.75.clone.1, s32[]{:T(128)S(6)} %select_n.111) | dynamic-update-slice | bytes 4718596 | tf_op jit(solution)/shard_map/dynamic_update_slice | solution.py:130
  1035.2 16.0 %dynamic_update_slice.28 = f32[3,2,8,64,1536]{4,3,2,1,0:T(8,128)} dynamic-update-slice(f32[3,2,8,64,1536]{4,3,2,1,0:T(8,128)} %dynamic_update_slice.27, f32[3,2,8,64,192]{4,3,2,1,0:T(8,128)} %collective-permute-done.3, s32[]{:T(128)} %constant.75.clone.1, s32[]{:T(128)} %constant.75.clone.1, s32[]{:T(128)} %constant.75.clone.1, s32[]{:T(128)} %constant.75.clone.1, s32[]{:T(128)S(6)} %select_n.113) | dynamic-update-slice | bytes 4718596 | tf_op jit(solution)/shard_map/dynamic_update_slice | solution.py:130
  1051.2 103.1 %collective-permute-done.4 = f32[3,2,8,64,192]{4,3,2,1,0:T(8,128)} collective-permute-done((f32[3,2,8,64,192]{4,3,2,1,0:T(8,128)}, f32[3,2,8,64,192]{4,3,2,1,0:T(8,128)}, u32[]{:S(2)}, u32[]{:S(2)}) %collective-permute-start.4) | collective-permute-done | bytes 2359328 | tf_op jit(solution)/shard_map/ppermute | solution.py:129
  1154.2 20.4 %dynamic_update_slice.29 = f32[3,2,8,64,1536]{4,3,2,1,0:T(8,128)} dynamic-update-slice(f32[3,2,8,64,1536]{4,3,2,1,0:T(8,128)} %dynamic_update_slice.28, f32[3,2,8,64,192]{4,3,2,1,0:T(8,128)} %collective-permute-done.4, s32[]{:T(128)} %constant.75.clone.1, s32[]{:T(128)} %constant.75.clone.1, s32[]{:T(128)} %constant.75.clone.1, s32[]{:T(128)} %constant.75.clone.1, s32[]{:T(128)S(6)} %select_n.115) | dynamic-update-slice | bytes 4718596 | tf_op jit(solution)/shard_map/dynamic_update_slice | solution.py:130
  1174.6 50.3 %collective-permute-done.5 = f32[3,2,8,64,192]{4,3,2,1,0:T(8,128)} collective-permute-done((f32[3,2,8,64,192]{4,3,2,1,0:T(8,128)}, f32[3,2,8,64,192]{4,3,2,1,0:T(8,128)}, u32[]{:S(2)}, u32[]{:S(2)}) %collective-permute-start.5) | collective-permute-done | bytes 2359328 | tf_op jit(solution)/shard_map/ppermute | solution.py:129
  1224.9 16.0 %dynamic_update_slice.30 = f32[3,2,8,64,1536]{4,3,2,1,0:T(8,128)} dynamic-update-slice(f32[3,2,8,64,1536]{4,3,2,1,0:T(8,128)} %dynamic_update_slice.29, f32[3,2,8,64,192]{4,3,2,1,0:T(8,128)} %collective-permute-done.5, s32[]{:T(128)} %constant.75.clone.1, s32[]{:T(128)} %constant.75.clone.1, s32[]{:T(128)} %constant.75.clone.1, s32[]{:T(128)} %constant.75.clone.1, s32[]{:T(128)S(6)} %select_n.117) | dynamic-update-slice | bytes 4718596 | tf_op jit(solution)/shard_map/dynamic_update_slice | solution.py:130
  1240.9 50.2 %collective-permute-done.6 = f32[3,2,8,64,192]{4,3,2,1,0:T(8,128)} collective-permute-done((f32[3,2,8,64,192]{4,3,2,1,0:T(8,128)}, f32[3,2,8,64,192]{4,3,2,1,0:T(8,128)}, u32[]{:S(2)}, u32[]{:S(2)}) %collective-permute-start.6) | collective-permute-done | bytes 2359328 | tf_op jit(solution)/shard_map/ppermute | solution.py:129
  1291.1 20.4 %dynamic_update_slice.31 = f32[3,2,8,64,1536]{4,3,2,1,0:T(8,128)} dynamic-update-slice(f32[3,2,8,64,1536]{4,3,2,1,0:T(8,128)} %dynamic_update_slice.30, f32[3,2,8,64,192]{4,3,2,1,0:T(8,128)} %collective-permute-done.6, s32[]{:T(128)} %constant.75.clone.1, s32[]{:T(128)} %constant.75.clone.1, s32[]{:T(128)} %constant.75.clone.1, s32[]{:T(128)} %constant.75.clone.1, s32[]{:T(128)S(6)} %select_n.119) | dynamic-update-slice | bytes 4718596 | tf_op jit(solution)/shard_map/dynamic_update_slice | solution.py:130
  1323.4 23.4 %fusion.31 = f32[1,2,8,64,1536]{4,3,2,1,0:T(8,128)} fusion(f32[3,2,8,64,1536]{4,3,2,1,0:T(8,128)} %dynamic_update_slice.31, f32[2,8,64,1536]{3,2,1,0:T(8,128)} %pad_maximum_fusion, f32[1536]{0:T(1024)S(1)} %get-tuple-element.7, f32[1536]{0:T(1024)S(1)} %get-tuple-element.8, f32[1536]{0:T(1024)S(1)} %get-tuple-element.3, f32[1536]{0:T(1024)S(1)} %get-tuple-element.4, ...), kind=kLoop, calls=%fused_computation.60 | loop fusion | flops 23592960 | bytes 18919424 | tf_op jit(solution)/shard_map/stack | solution.py:135
  1353.1 104.9 %fusion.9 = f32[2,2,8,96,1536]{4,3,2,1,0:T(8,128)} fusion(f32[1,2,8,64,1536]{4,3,2,1,0:T(8,128)} %maximum_bitcast_fusion, f32[1,2,8,64,1536]{4,3,2,1,0:T(8,128)} %fusion.31, f32[1,2,8,96,1536]{4,3,2,1,0:T(8,128)} %bitcast.85, f32[1,2,8,96,1536]{4,3,2,1,0:T(8,128)} %bitcast.86, f32[2,2,8,32,1536]{4,3,2,1,0:T(8,128)} %fusion.28, f32[96]{0:T(128)S(1)} %pad.6.clone, ...), kind=kOutput, calls=%fused_computation.26 | convolution fusion | flops 87015555072 | bytes 66063744 | tf_op jit(solution)/shard_map/fpkqy,yj->fpkqj/dot_general | solution.py:146
  1458.0 99.2 %fusion.19 = f32[2,2,8,96,1536]{4,3,2,1,0:T(8,128)} fusion(f32[2,2,8,96,1536]{4,3,2,1,0:T(8,128)} %fusion.9, f32[1536,1536]{1,0:T(8,128)} %param.15, f32[8,96,1536]{2,1,0:T(8,128)} %broadcast_add_fusion), kind=kOutput, calls=%fused_computation.36 | convolution fusion | flops 86977806336 | bytes 51904512 | tf_op jit(solution)/shard_map/fpkqj,yj->fpkqy/dot_general | solution.py:150
  1557.2 12.6 slice_bitcast_fusion
  (39 shorter events, 34.7 us)
Async XLA Ops:
  0.6 19.5 %copy-start = (bf16[3,192,24,512]{3,2,1,0:T(8,128)(2,1)S(1)}, bf16[3,192,24,512]{3,2,1,0:T(8,128)(2,1)}, u32[]{:S(2)}) copy-start(bf16[3,192,24,512]{3,2,1,0:T(8,128)(2,1)} %param.9) | copy-start | bytes 42467332
  151.9 418.1 %all-to-all-start = ((f32[3,192,24,512]{1,2,0,3:T(8,128)}), f32[3,192,24,512]{1,2,0,3:T(8,128)}, u32[]{:S(2)}, u32[]{:S(2)}) async-start(f32[3,192,24,512]{1,2,0,3:T(8,128)} %copy.22), calls=%async_computation | async-start | bytes 75497472 | tf_op jit(solution)/shard_map/all_to_all | solution.py:105
  746.1 11.1 collective-permute-start
  746.2 202.5 %collective-permute-start.1 = (f32[3,2,8,64,192]{4,3,2,1,0:T(8,128)}, f32[3,2,8,64,192]{4,3,2,1,0:T(8,128)}, u32[]{:S(2)}, u32[]{:S(2)}) collective-permute-start(f32[3,2,8,64,192]{4,3,2,1,0:T(8,128)} %get-tuple-element.20), channel_id=1, source_target_pairs={{0,2},{1,3},{2,0},{3,1},{4,6},{5,7},{6,4},{7,5},{8,10},{9,11},{10,... | collective-permute-start | bytes 7077896 | tf_op jit(solution)/shard_map/ppermute | solution.py:129
  747.9 267.7 %collective-permute-start.2 = (f32[3,2,8,64,192]{4,3,2,1,0:T(8,128)}, f32[3,2,8,64,192]{4,3,2,1,0:T(8,128)}, u32[]{:S(2)}, u32[]{:S(2)}) collective-permute-start(f32[3,2,8,64,192]{4,3,2,1,0:T(8,128)} %get-tuple-element.21), channel_id=1, source_target_pairs={{0,3},{1,2},{2,1},{3,0},{4,7},{5,6},{6,5},{7,4},{8,11},{9,10},{10,... | collective-permute-start | bytes 7077896 | tf_op jit(solution)/shard_map/ppermute | solution.py:129
  748.1 200.8 %copy-start.3 = (s32[8,96]{1,0:T(8,128)S(1)}, s32[8,96]{1,0:T(8,128)}, u32[]{:S(2)}) copy-start(s32[8,96]{1,0:T(8,128)} %param.12) | copy-start | bytes 9220
  748.1 200.9 %copy-start.1 = (f32[7,1536]{1,0:T(8,128)S(1)}, f32[7,1536]{1,0:T(8,128)}, u32[]{:S(2)}) copy-start(f32[7,1536]{1,0:T(8,128)} %param.13) | copy-start | bytes 129028
  748.1 201.2 %copy-start.2 = (f32[1536]{0:T(1024)S(1)}, f32[1536]{0:T(1024)}, u32[]{:S(2)}) copy-start(f32[1536]{0:T(1024)} %param.14) | copy-start | bytes 18436
  748.1 287.1 %collective-permute-start.3 = (f32[3,2,8,64,192]{4,3,2,1,0:T(8,128)}, f32[3,2,8,64,192]{4,3,2,1,0:T(8,128)}, u32[]{:S(2)}, u32[]{:S(2)}) collective-permute-start(f32[3,2,8,64,192]{4,3,2,1,0:T(8,128)} %get-tuple-element.22), channel_id=1, source_target_pairs={{0,4},{1,5},{2,6},{3,7},{4,0},{5,1},{6,2},{7,3},{8,12},{9,13},{10,... | collective-permute-start | bytes 7077896 | tf_op jit(solution)/shard_map/ppermute | solution.py:129
  754.9 399.4 %collective-permute-start.4 = (f32[3,2,8,64,192]{4,3,2,1,0:T(8,128)}, f32[3,2,8,64,192]{4,3,2,1,0:T(8,128)}, u32[]{:S(2)}, u32[]{:S(2)}) collective-permute-start(f32[3,2,8,64,192]{4,3,2,1,0:T(8,128)} %get-tuple-element.24), channel_id=1, source_target_pairs={{0,5},{1,4},{2,7},{3,6},{4,1},{5,0},{6,3},{7,2},{8,13},{9,12},{10,... | collective-permute-start | bytes 7077896 | tf_op jit(solution)/shard_map/ppermute | solution.py:129
  757.3 467.7 %collective-permute-start.5 = (f32[3,2,8,64,192]{4,3,2,1,0:T(8,128)}, f32[3,2,8,64,192]{4,3,2,1,0:T(8,128)}, u32[]{:S(2)}, u32[]{:S(2)}) collective-permute-start(f32[3,2,8,64,192]{4,3,2,1,0:T(8,128)} %get-tuple-element.23), channel_id=1, source_target_pairs={{0,6},{1,7},{2,4},{3,5},{4,2},{5,3},{6,0},{7,1},{8,14},{9,15},{10,... | collective-permute-start | bytes 7077896 | tf_op jit(solution)/shard_map/ppermute | solution.py:129
  948.7 342.4 %collective-permute-start.6 = (f32[3,2,8,64,192]{4,3,2,1,0:T(8,128)}, f32[3,2,8,64,192]{4,3,2,1,0:T(8,128)}, u32[]{:S(2)}, u32[]{:S(2)}) collective-permute-start(f32[3,2,8,64,192]{4,3,2,1,0:T(8,128)} %get-tuple-element.17), channel_id=1, source_target_pairs={{0,7},{1,6},{2,5},{3,4},{4,3},{5,2},{6,1},{7,0},{8,15},{9,14},{10,... | collective-permute-start | bytes 7077896 | tf_op jit(solution)/shard_map/ppermute | solution.py:129
